TPU v7x, 32 devices: a whole 2x2x4 slice. The times are simulated.
32 devices in a mesh: groups: 2 (over x), section: 2 (over core), tensor: 8 (over z, y).
Axes of the slice: x: 2, y: 2, z: 4, core: 2. Of those that a mesh axis runs over, the one named last changes fastest.
Arguments:
- hidden: bfloat16 [2, 1024, 26624], P('section', 'groups', 'tensor'), parts along dimension 1, may hold values from -6 to 6
- down_weight: bfloat16 [2, 26624, 8192], P('section', 'tensor'), may hold values from -0.0546875 to 0.0546875
- residual: bfloat16 [2, 1024, 8192], P('section', 'groups', 'tensor'), parts along dimension 1, may hold values from -100 to 100
- norm_gain: float32 [2, 8192], P('section'), may hold values from 0.1 to 1.9
- qkv_weight: bfloat16 [2, 8192, 9216], P('section', None, 'tensor'), may hold values from -0.0625 to 0.0625
Outputs:
- received: bfloat16 [2, 1024, 8192], P('section', 'groups', 'tensor'), parts along dimension 1
- projected: bfloat16 [2, 1024, 9216], P('section', 'groups', 'tensor'), parts along dimension 1
There are 2 independent parts, one for each index of `groups`. A program takes and returns all parts, laid end to end along the dimension named above; an argument that names none is the same for every part. Nothing has to cross between parts.
All inputs are finite; a program needn't handle non-finite values.
Results may differ from a plain program's by a relative error of at most 0.0057.
Values may be sent and summed in bfloat16 or wider, within the bound.
No kernel may reach another device: no remote copies, remote signals or barrier semaphores. Data moves between devices by JAX's collectives and lax.ppermute only.
A program may use at most 192 MiB of HBM per device.

v0:
```python
import jax
import jax.numpy as jnp
from jax import lax
from jax.sharding import PartitionSpec as P

D = 8192
epsilon = 1e-05


def shifted(value, axis, steps):
    count = lax.axis_size(axis)
    pairs = [(source, (source + steps) % count) for source in range(count)]
    return lax.ppermute(value, axis, pairs)


def normalize(floats, gain_part):
    square_sum = jnp.sum(floats * floats, axis=1, keepdims=True)
    scale_inv = lax.rsqrt(square_sum / D + epsilon)
    return (floats * scale_inv * gain_part[None, :]).astype(jnp.bfloat16)


def body(hidden, down_weight, residual, norm_gain, qkv_weight):
    hidden_local = hidden[0]
    down_local = down_weight[0]
    residual_local = residual[0]
    gain_full = norm_gain[0]
    qkv_local = qkv_weight[0]
    partial_sum = jnp.dot(hidden_local, down_local, preferred_element_type=jnp.float32)
    summed = lax.psum_scatter(partial_sum, "tensor", scatter_dimension=1, tiled=True)
    stream = (residual_local.astype(jnp.float32) + summed).astype(jnp.bfloat16)
    received = shifted(stream, "section", 1)
    gathered = lax.all_gather(received, "tensor", axis=1, tiled=True)
    normed = normalize(gathered.astype(jnp.float32), gain_full)
    projected = jnp.dot(normed, qkv_local, preferred_element_type=jnp.float32).astype(jnp.bfloat16)
    return (received[None], projected[None])


def solution(mesh):
    placed = (
        P("section", "groups", "tensor"),
        P("section", "tensor", None),
        P("section", "groups", "tensor"),
        P("section", None),
        P("section", None, "tensor"),
    )
    return jax.shard_map(
        body,
        mesh=mesh,
        in_specs=placed,
        out_specs=(P("section", "groups", "tensor"), P("section", "groups", "tensor")),
        check_vma=False,
    )
```

profile of v0, /device:TPU:0, one launch (start us, length us, event | category | flops | bytes accessed | tf_op | source)
XLA Modules:
  0.0 487.6 jit_solution(3447809766854134224)
XLA Ops:
  7.2 0.0 copy-start
  7.2 0.0 reduce-scatter.2.cloned.1.call-start
  7.2 1.9 copy-done
  9.1 35.6 %fusion = f32[512,8192]{1,0:T(8,128)} fusion(bf16[1,3328,8192]{2,1,0:T(8,128)(2,1)} %param.6, bf16[1,512,3328]{2,1,0:T(8,128)(2,1)S(1)} %copy-done), kind=kOutput, calls=%fused_computation | convolution fusion | flops 27917287424 | bytes 74711040 | tf_op jit(solution)/shard_map/dot_general | solution.py:28
  44.7 0.0 copy-start.4
  44.7 0.0 copy-start.5
  44.7 0.0 reduce-scatter.2.cloned.1.call-update
  44.7 0.0 all-gather.2.cloned.1.call-start
  44.8 283.0 %reduce-scatter.2.cloned.1.call-done = f32[512,1024]{1,0:T(8,128)} async-done(((f32[512,8192]{1,0:T(8,128)}), f32[512,1024]{1,0:T(8,128)}) %reduce-scatter.2.cloned.1.call-update) | async-done | bytes 2097168 | tf_op jit(solution)/shard_map/reduce_scatter | solution.py:29
  327.8 0.0 copy-done.4
  327.8 1.9 fusion.21
  329.8 0.1 collective-permute-start
  329.8 2.6 collective-permute-done
  332.5 0.0 copy-start.2
  332.5 1.0 copy-done.2
  333.5 0.0 all-gather.2.cloned.1.call-update
  333.5 123.7 %all-gather.2.cloned.1.call-done = bf16[512,8192]{1,0:T(8,128)(2,1)} async-done(((bf16[512,1024]{1,0:T(8,128)(2,1)}), bf16[512,8192]{1,0:T(8,128)(2,1)}) %all-gather.2.cloned.1.call-update) | async-done | bytes 8388624 | tf_op jit(solution)/shard_map/all_gather | solution.py:32
  457.2 5.1 %fusion.4 = f32[512]{0:T(512)S(1)} fusion(bf16[512,8192]{1,0:T(8,128)(2,1)} %all-gather.2.cloned.1.call-done), kind=kLoop, calls=%fused_computation.6 | loop fusion | flops 12582400 | bytes 8390656 | tf_op jit(solution)/shard_map/reduce_sum | solution.py:17
  462.3 0.0 copy-done.5
  462.3 0.0 copy-start.3
  462.3 0.0 copy-start.1
  462.3 17.5 %fusion.16 = bf16[1,512,1152]{2,1,0:T(8,128)(2,1)} fusion(bf16[1,8192,1152]{2,1,0:T(8,128)(2,1)} %param.9, bf16[512,8192]{1,0:T(8,128)(2,1)} %all-gather.2.cloned.1.call-done, f32[8192]{0:T(1024)S(1)} %bitcast.21, f32[512]{0:T(512)S(1)} %add_rsqrt_fusion), kind=kOutput, calls=%fused_computation.13 | convolution fusion | flops 9681043456 | bytes 28477440 | tf_op jit(solution)/shard_map/dot_general | solution.py:34
  479.8 0.0 copy-done.3
  479.8 1.0 copy.8
  480.8 0.0 copy-done.1
  (1 shorter events, 0.0 us)
Async XLA Ops:
  7.2 2.0 copy-start
  7.2 320.6 %reduce-scatter.2.cloned.1.call-start = ((), (), s32[]{:S(2)}) async-start(), calls=%async_computation.1 | async-start | bytes 18874368 | tf_op jit(solution)/shard_map/reduce_scatter | solution.py:29
  44.7 283.1 %copy-start.4 = (bf16[1,512,1024]{2,1,0:T(8,128)(2,1)S(1)}, bf16[1,512,1024]{2,1,0:T(8,128)(2,1)}, u32[]{:S(2)}) copy-start(bf16[1,512,1024]{2,1,0:T(8,128)(2,1)} %param.7) | copy-start | bytes 3145732
  44.7 417.6 %copy-start.5 = (f32[1,8192]{1,0:T(1,128)S(1)}, f32[1,8192]{1,0:T(1,128)}, u32[]{:S(2)}) copy-start(f32[1,8192]{1,0:T(1,128)} %param.8) | copy-start | bytes 98308
  44.7 412.4 %all-gather.2.cloned.1.call-start = ((), (), s32[]{:S(2)}) async-start(), calls=%async_computation.2 | async-start | bytes 9437184 | tf_op jit(solution)/shard_map/all_gather | solution.py:32
  329.8 2.7 collective-permute-start
  332.5 1.0 copy-start.2
  462.3 17.5 %copy-start.3 = (bf16[512,1024]{1,0:T(8,128)(2,1)S(1)}, bf16[512,1024]{1,0:T(8,128)(2,1)}, u32[]{:S(2)}) copy-start(bf16[512,1024]{1,0:T(8,128)(2,1)} %copy-done.2) | copy-start | bytes 3145732
  462.3 18.5 %copy-start.1 = (bf16[1,512,3328]{2,1,0:T(8,128)(2,1)S(1)}, bf16[1,512,3328]{2,1,0:T(8,128)(2,1)}, u32[]{:S(2)}) copy-start(bf16[1,512,3328]{2,1,0:T(8,128)(2,1)} %param.5) | copy-start | bytes 10223620
Sparse Core Ops, SparseCore 0:
  44.9 282.9 reduce-scatter.1
  333.6 123.5 all-gather.1
where the time goes:
time: 488 us
  waiting for transfers between devices  409 us (84%)
  matrix products  53 us (11%)
  between operations  14.1 us (3%)
  other arithmetic  7.05 us (1%)
    reduce_scatter x1, waiting for transfers between devices, body(): lax.psum_scatter(partial_sum, 'tensor', scatter_dimension=1, tiled=True)  283 us
    all_gather x1, waiting for transfers between devices, body(): gathered = lax.all_gather(received, 'tensor', axis=1, tiled=True)  124 us
    dot_general x1, matrix products, body(): jnp.dot(hidden_local, down_local, preferred_element_type=jnp.float32)  35.6 us
    dot_general x1, matrix products, body(): jnp.dot(normed, qkv_local, preferred_element_type=jnp.float32)  17.5 us
  transfers between devices with their start and end apart: 3, of which 3 were waited for; matrix products, arithmetic and copies ran while one was open for 0% of the time, Pallas kernels for 0%

commit v1 on v0

--- a/solution.py
+++ b/solution.py
@@ -5,6 +5,29 @@
 
 D = 8192
 epsilon = 1e-05
+
+
+def apply_views(q_in, axis_no):
+    arr_out = jax.lax.psum(1, "tensor")
+    e_now = jax.lax.axis_index("tensor")
+    k_now, finding, val2 = (arr_out, e_now, q_in.shape[axis_no])
+    log = tuple(((t, (t + 1) % k_now) for t in range(k_now)))
+    rack = tuple(((t, (t - 1) % k_now) for t in range(k_now)))
+    r_now = jnp.zeros((*q_in.shape[:axis_no], k_now * val2, *q_in.shape[axis_no + 1 :]), q_in.dtype)
+    r_now = lax.dynamic_update_slice_in_dim(r_now, q_in, finding * val2, axis=axis_no)
+    f_next = row_out = q_in
+    parts_out = k_now // 2
+    for idx in [*range(1, parts_out + 1)]:
+        f_next = jax.lax.ppermute(f_next, axis_name="tensor", perm=log)
+        r_now = lax.dynamic_update_slice_in_dim(
+            r_now, f_next, (finding - idx) % k_now * val2, axis=axis_no
+        )
+        if idx < k_now - parts_out:
+            row_out = jax.lax.ppermute(row_out, "tensor", perm=rack)
+            r_now = lax.dynamic_update_slice_in_dim(
+                r_now, row_out, (finding + idx) % k_now * val2, axis=axis_no
+            )
+    return r_now
 
 
 def shifted(value, axis, steps):
@@ -29,7 +52,7 @@
     summed = lax.psum_scatter(partial_sum, "tensor", scatter_dimension=1, tiled=True)
     stream = (residual_local.astype(jnp.float32) + summed).astype(jnp.bfloat16)
     received = shifted(stream, "section", 1)
-    gathered = lax.all_gather(received, "tensor", axis=1, tiled=True)
+    gathered = apply_views(received, 1)
     normed = normalize(gathered.astype(jnp.float32), gain_full)
     projected = jnp.dot(normed, qkv_local, preferred_element_type=jnp.float32).astype(jnp.bfloat16)
     return (received[None], projected[None])

time: 488 us -> 526 us (1.078)
  waiting for transfers between devices: 409 us -> 430 us
  starting transfers between devices: 0.15 us -> 16.9 us
  local copies, waits for them, and re-layouts: 3.88 us -> 9.69 us
    ppermute x0 -> x7, waiting for transfers between devices: none -> 144 us  [the longest x4 144 us: apply_views(): f_next = jax.lax.ppermute(f_next, axis_name='tensor', perm=log)]
    all_gather x1 -> x0, waiting for transfers between devices: 124 us -> none  [body(): gathered = lax.all_gather(received, 'tensor', axis=1, tiled=True)]
    ppermute x0 -> x7, starting transfers between devices: none -> 16.8 us  [the longest x4 9 us: apply_views(): f_next = jax.lax.ppermute(f_next, axis_name='tensor', perm=log)]
    dynamic_update_slice x0 -> x8, local copies, waits for them, and re-layouts: none -> 5.77 us  [the longest x4 2.89 us: apply_views(): lax.dynamic_update_slice_in_dim(r_now, f_next, (finding - idx) % k_now *...]
  transfers between devices with their start and end apart: 3 -> 9, of which waited for: 3 -> 6; matrix products, arithmetic and copies ran while one was open for 0% -> 1% of each run, Pallas kernels for 0% -> 0%
where the time goes in v1:
time: 526 us; the launch traced here: 525 us
  waiting for transfers between devices  430 us (82%)
  matrix products  51.1 us (10%)
  starting transfers between devices  16.9 us (3%)
  between operations  14.2 us (3%)
  local copies, waits for them, and re-layouts  9.69 us (2%)
    reduce_scatter x1, waiting for transfers between devices, body(): lax.psum_scatter(partial_sum, 'tensor', scatter_dimension=1, tiled=True)  283 us
    ppermute x4, waiting for transfers between devices, apply_views(): f_next = jax.lax.ppermute(f_next, axis_name='tensor', perm=log)  144 us
    dot_general x1, matrix products, body(): jnp.dot(hidden_local, down_local, preferred_element_type=jnp.float32)  35.6 us
    dot_general x1, matrix products, body(): jnp.dot(normed, qkv_local, preferred_element_type=jnp.float32)  15.5 us
  transfers between devices with their start and end apart: 9, of which 6 were waited for; matrix products, arithmetic and copies ran while one was open for 1% of the time, Pallas kernels for 0%

profile of v1, /device:TPU:0, one launch (start us, length us, event | category | flops | bytes accessed | tf_op | source)
XLA Modules:
  0.0 525.4 jit_solution(6086670701055181917)
XLA Ops:
  7.2 0.0 copy-start
  7.2 0.0 reduce-scatter.2.cloned.1.call-start
  7.2 1.9 copy-done
  9.1 35.6 %fusion = f32[512,8192]{1,0:T(8,128)} fusion(bf16[1,3328,8192]{2,1,0:T(8,128)(2,1)} %param.6, bf16[1,512,3328]{2,1,0:T(8,128)(2,1)S(1)} %copy-done), kind=kOutput, calls=%fused_computation | convolution fusion | flops 27917287424 | bytes 74711040 | tf_op jit(solution)/shard_map/dot_general | solution.py:51
  44.7 0.0 copy-start.6
  44.7 0.0 reduce-scatter.2.cloned.1.call-update
  44.7 283.1 %reduce-scatter.2.cloned.1.call-done = f32[512,1024]{1,0:T(8,128)} async-done(((f32[512,8192]{1,0:T(8,128)}), f32[512,1024]{1,0:T(8,128)}) %reduce-scatter.2.cloned.1.call-update) | async-done | bytes 2097168 | tf_op jit(solution)/shard_map/reduce_scatter | solution.py:52
  327.8 0.0 copy-done.6
  327.8 1.9 fusion.21
  329.8 0.1 collective-permute-start
  329.9 2.6 collective-permute-done
  332.5 0.0 copy-start.2
  332.5 1.5 collective-permute-start.1
  334.0 3.3 collective-permute-start.2
  337.2 41.9 %collective-permute-done.1 = bf16[512,1024]{1,0:T(8,128)(2,1)S(1)} collective-permute-done((bf16[512,1024]{1,0:T(8,128)(2,1)S(1)}, bf16[512,1024]{1,0:T(8,128)(2,1)S(1)}, u32[]{:S(2)}, u32[]{:S(2)}) %collective-permute-start.1) | collective-permute-done | bytes 1048608 | tf_op jit(solution)/shard_map/ppermute | solution.py:21
  379.2 2.5 collective-permute-start.3
  381.6 0.0 collective-permute-done.2
  381.6 2.2 collective-permute-start.4
  383.9 42.1 %collective-permute-done.3 = bf16[512,1024]{1,0:T(8,128)(2,1)S(1)} collective-permute-done((bf16[512,1024]{1,0:T(8,128)(2,1)S(1)}, bf16[512,1024]{1,0:T(8,128)(2,1)S(1)}, u32[]{:S(2)}, u32[]{:S(2)}) %collective-permute-start.3) | collective-permute-done | bytes 1048608 | tf_op jit(solution)/shard_map/ppermute | solution.py:21
  426.0 0.0 copy-start.4
  426.0 2.5 collective-permute-start.5
  428.5 0.0 collective-permute-done.4
  428.5 0.0 copy-done.4
  428.5 2.2 collective-permute-start.6
  430.7 41.9 %collective-permute-done.5 = bf16[512,1024]{1,0:T(8,128)(2,1)} collective-permute-done((bf16[512,1024]{1,0:T(8,128)(2,1)S(1)}, bf16[512,1024]{1,0:T(8,128)(2,1)}, u32[]{:S(2)}, u32[]{:S(2)}) %collective-permute-start.5) | collective-permute-done | bytes 1048608 | tf_op jit(solution)/shard_map/ppermute | solution.py:21
  472.6 2.6 collective-permute-start.7
  475.2 0.0 copy-start.5
  475.2 1.0 broadcast_in_dim.11
  476.2 0.1 constant_dynamic-update-slice_fusion.7
  476.3 0.1 constant_dynamic-update-slice_fusion.6
  476.4 0.1 constant_dynamic-update-slice_fusion.5
  476.6 0.0 copy-done.5
  476.6 0.1 constant_dynamic-update-slice_fusion.4
  476.7 0.0 copy-done.2
  476.7 0.0 copy-start.7
  476.7 1.3 constant_dynamic-update-slice_fusion.3
  478.1 1.3 constant_dynamic-update-slice_fusion.2
  479.4 0.0 collective-permute-done.6
  479.4 1.3 constant_dynamic-update-slice_fusion.1
  480.8 18.2 %collective-permute-done.7 = bf16[512,1024]{1,0:T(8,128)(2,1)} collective-permute-done((bf16[512,1024]{1,0:T(8,128)(2,1)}, bf16[512,1024]{1,0:T(8,128)(2,1)}, u32[]{:S(2)}, u32[]{:S(2)}) %collective-permute-start.7) | collective-permute-done | bytes 1048608 | tf_op jit(solution)/shard_map/ppermute | solution.py:21
  498.9 1.3 constant_dynamic-update-slice_fusion
  500.3 1.7 fusion.4
  502.0 0.0 copy-done.7
  502.0 0.0 copy-start.3
  502.0 0.0 copy-start.1
  502.0 15.5 %fusion.16 = bf16[1,512,1152]{2,1,0:T(8,128)(2,1)} fusion(bf16[1,8192,1152]{2,1,0:T(8,128)(2,1)} %param.9, bf16[512,8192]{1,0:T(8,128)(2,1)S(1)} %constant_dynamic-update-slice_fusion, f32[8192]{0:T(1024)S(1)} %bitcast.21, f32[512]{0:T(512)S(1)} %add_rsqrt_fusion), kind=kOutput, calls=%fused_computation.13 | convolution fusion | flops 9681043456 | bytes 28477440 | tf_op jit(solution)/shard_map/dot_general | solution.py:57
  517.5 0.0 copy-done.3
  517.5 1.0 copy.16
  518.5 0.0 copy-done.1
  (1 shorter events, 0.0 us)
Async XLA Ops:
  7.2 2.0 copy-start
  7.2 320.7 %reduce-scatter.2.cloned.1.call-start = ((), (), s32[]{:S(2)}) async-start(), calls=%async_computation.1 | async-start | bytes 18874368 | tf_op jit(solution)/shard_map/reduce_scatter | solution.py:52
  44.7 283.1 %copy-start.6 = (bf16[1,512,1024]{2,1,0:T(8,128)(2,1)S(1)}, bf16[1,512,1024]{2,1,0:T(8,128)(2,1)}, u32[]{:S(2)}) copy-start(bf16[1,512,1024]{2,1,0:T(8,128)(2,1)} %param.7) | copy-start | bytes 3145732
  329.8 2.7 collective-permute-start
  332.5 144.2 %copy-start.2 = (bf16[512,1024]{1,0:T(8,128)(2,1)}, bf16[512,1024]{1,0:T(8,128)(2,1)S(1)}, u32[]{:S(2)}) copy-start(bf16[512,1024]{1,0:T(8,128)(2,1)S(1)} %collective-permute-done) | copy-start | bytes 3145732
  332.5 46.6 %collective-permute-start.1 = (bf16[512,1024]{1,0:T(8,128)(2,1)S(1)}, bf16[512,1024]{1,0:T(8,128)(2,1)S(1)}, u32[]{:S(2)}, u32[]{:S(2)}) collective-permute-start(bf16[512,1024]{1,0:T(8,128)(2,1)S(1)} %collective-permute-done), channel_id=1, source_target_pairs={{0,1},{1,2},{2,3},{3,4},{4,5},{5,6},{6,7},{7,0},{8,9},{9,10},{10,1... | collective-permute-start | bytes 3145736 | tf_op jit(solution)/shard_map/ppermute | solution.py:21
  334.0 47.7 %collective-permute-start.2 = (bf16[512,1024]{1,0:T(8,128)(2,1)S(1)}, bf16[512,1024]{1,0:T(8,128)(2,1)S(1)}, u32[]{:S(2)}, u32[]{:S(2)}) collective-permute-start(bf16[512,1024]{1,0:T(8,128)(2,1)S(1)} %collective-permute-done), channel_id=1, source_target_pairs={{0,7},{1,0},{2,1},{3,2},{4,3},{5,4},{6,5},{7,6},{8,15},{9,8},{10,9... | collective-permute-start | bytes 3145736 | tf_op jit(solution)/shard_map/ppermute | solution.py:26
  379.2 46.8 %collective-permute-start.3 = (bf16[512,1024]{1,0:T(8,128)(2,1)S(1)}, bf16[512,1024]{1,0:T(8,128)(2,1)S(1)}, u32[]{:S(2)}, u32[]{:S(2)}) collective-permute-start(bf16[512,1024]{1,0:T(8,128)(2,1)S(1)} %collective-permute-done.1), channel_id=1, source_target_pairs={{0,1},{1,2},{2,3},{3,4},{4,5},{5,6},{6,7},{7,0},{8,9},{9,10},{10,1... | collective-permute-start | bytes 3145736 | tf_op jit(solution)/shard_map/ppermute | solution.py:21
  381.6 46.8 %collective-permute-start.4 = (bf16[512,1024]{1,0:T(8,128)(2,1)S(1)}, bf16[512,1024]{1,0:T(8,128)(2,1)}, u32[]{:S(2)}, u32[]{:S(2)}) collective-permute-start(bf16[512,1024]{1,0:T(8,128)(2,1)S(1)} %collective-permute-done.2), channel_id=1, source_target_pairs={{0,7},{1,0},{2,1},{3,2},{4,3},{5,4},{6,5},{7,6},{8,15},{9,8},{10,9... | collective-permute-start | bytes 3145736 | tf_op jit(solution)/shard_map/ppermute | solution.py:26
  426.0 2.5 copy-start.4
  426.0 46.6 %collective-permute-start.5 = (bf16[512,1024]{1,0:T(8,128)(2,1)S(1)}, bf16[512,1024]{1,0:T(8,128)(2,1)}, u32[]{:S(2)}, u32[]{:S(2)}) collective-permute-start(bf16[512,1024]{1,0:T(8,128)(2,1)S(1)} %collective-permute-done.3), channel_id=1, source_target_pairs={{0,1},{1,2},{2,3},{3,4},{4,5},{5,6},{6,7},{7,0},{8,9},{9,10},{10,1... | collective-permute-start | bytes 3145736 | tf_op jit(solution)/shard_map/ppermute | solution.py:21
  428.5 50.9 %collective-permute-start.6 = (bf16[512,1024]{1,0:T(8,128)(2,1)}, bf16[512,1024]{1,0:T(8,128)(2,1)}, u32[]{:S(2)}, u32[]{:S(2)}) collective-permute-start(bf16[512,1024]{1,0:T(8,128)(2,1)} %collective-permute-done.4), channel_id=1, source_target_pairs={{0,7},{1,0},{2,1},{3,2},{4,3},{5,4},{6,5},{7,6},{8,15},{9,8},{10,9... | collective-permute-start | bytes 3145736 | tf_op jit(solution)/shard_map/ppermute | solution.py:26
  472.6 26.3 %collective-permute-start.7 = (bf16[512,1024]{1,0:T(8,128)(2,1)}, bf16[512,1024]{1,0:T(8,128)(2,1)}, u32[]{:S(2)}, u32[]{:S(2)}) collective-permute-start(bf16[512,1024]{1,0:T(8,128)(2,1)} %collective-permute-done.5), channel_id=1, source_target_pairs={{0,1},{1,2},{2,3},{3,4},{4,5},{5,6},{6,7},{7,0},{8,9},{9,10},{10,1... | collective-permute-start | bytes 3145736 | tf_op jit(solution)/shard_map/ppermute | solution.py:21
  475.2 1.4 copy-start.5
  476.7 25.3 %copy-start.7 = (f32[1,8192]{1,0:T(1,128)S(1)}, f32[1,8192]{1,0:T(1,128)}, u32[]{:S(2)}) copy-start(f32[1,8192]{1,0:T(1,128)} %param.8) | copy-start | bytes 98308
  502.0 15.5 %copy-start.3 = (bf16[512,1024]{1,0:T(8,128)(2,1)S(1)}, bf16[512,1024]{1,0:T(8,128)(2,1)}, u32[]{:S(2)}) copy-start(bf16[512,1024]{1,0:T(8,128)(2,1)} %copy-done.2) | copy-start | bytes 3145732
  502.0 16.5 %copy-start.1 = (bf16[1,512,3328]{2,1,0:T(8,128)(2,1)S(1)}, bf16[1,512,3328]{2,1,0:T(8,128)(2,1)}, u32[]{:S(2)}) copy-start(bf16[1,512,3328]{2,1,0:T(8,128)(2,1)} %param.5) | copy-start | bytes 10223620
Sparse Core Ops, SparseCore 0:
  44.9 282.9 reduce-scatter.1
